TPU v7x, 128 devices: a whole 4x4x4 slice. The times are simulated.
128 devices in a mesh: rows: 32 (over x, y, core), eig: 4 (over z).
Axes of the slice: x: 4, y: 4, z: 4, core: 2. Of those that a mesh axis runs over, the one named last changes fastest.
Arguments:
- phi_obs: bfloat16 [16384, 4096], P('rows', 'eig'), may hold values from -0.09375 to 0.09375
- counts: int32 [32], P('rows'), may hold values from 1 to 512, as said below
- targets: bfloat16 [16384, 128], P('rows', 'eig'), may hold values from -6 to 6
- spectrum: float32 [4096], replicated, may hold values from 0.1 to 10
- coef_noise: float32 [4096, 128], replicated, may hold values from -6 to 6
- phi_slab: bfloat16 [65536, 4096], P('rows', 'eig'), may hold values from -0.09375 to 0.09375
Outputs:
- factor: float32 [4096, 4096], P('rows', 'eig')
- solved: float32 [4096, 128], P('rows', 'eig')
- slab_prior: float32 [65536, 128], P(('rows', 'eig'))
Inputs may be any that keep to these rules, and one draw needn't show every extreme that they name: counts[r] is the number of live rows of shard r, which come first in the shard; some shard is full (512).
All inputs are finite; a program needn't handle non-finite values.
Results may differ from a plain program's by a relative error of at most 0.0029.
Values may be sent and summed in bfloat16 or wider, within the bound.
No kernel may reach another device: no remote copies, remote signals or barrier semaphores. Data moves between devices by JAX's collectives and lax.ppermute only.
A program may use at most 192 MiB of HBM per device.

v0:
```python
import jax
import jax.numpy as jnp
from jax import lax
from jax.sharding import PartitionSpec as P

PANEL = 512
ROW_BLOCK = 256


def from_root(array, axis, root):
    mine = lax.axis_index(axis) == root
    return lax.psum(jnp.where(mine, array, jnp.zeros_like(array)), axis)


def panel_factor_rows(head, panel_rows, row_ids):
    solved_rows = jax.scipy.linalg.solve_triangular(head, panel_rows.T, lower=True).T
    head_rows = jnp.take(head, jnp.clip(row_ids, 0, head.shape[0] - 1), axis=0)
    return jnp.where(row_ids[:, None] < head.shape[0], head_rows, solved_rows)


def on_device(phi_obs, counts, targets, spectrum, coef_noise, phi_slab):
    rows_total = lax.axis_size("rows")
    eig_total = lax.axis_size("eig")
    row_index = lax.axis_index("rows")
    eig_index = lax.axis_index("eig")
    obs_slots, width_dev = phi_obs.shape
    order = width_dev * eig_total
    row_share = order // rows_total
    sample_share = targets.shape[1]
    position = jnp.arange(obs_slots, dtype=jnp.int32)
    own_count = counts[0]
    local_rows = phi_obs
    local_targets = targets
    keep = (position < own_count).astype(jnp.bfloat16)[:, None]
    local_rows = local_rows * keep
    local_targets = local_targets * keep
    full_rows = lax.all_gather(local_rows, "eig", axis=1, tiled=True)
    block_count = (own_count + ROW_BLOCK - 1) // ROW_BLOCK

    def add_block(block, total_sum):
        left = lax.dynamic_slice(full_rows, (block * ROW_BLOCK, 0), (ROW_BLOCK, order))
        right = lax.dynamic_slice_in_dim(local_rows, block * ROW_BLOCK, ROW_BLOCK, 0)
        return total_sum + lax.dot_general(
            left, right, (((0,), (0,)), ((), ())), preferred_element_type=jnp.float32
        )

    gram_columns = lax.psum(
        lax.fori_loop(0, block_count, add_block, jnp.zeros((order, width_dev), jnp.float32)), "rows"
    )
    gram_block = lax.dynamic_slice_in_dim(gram_columns, row_index * row_share, row_share, 0)
    rhs_part = lax.dot_general(
        full_rows, local_targets, (((0,), (0,)), ((), ())), preferred_element_type=jnp.float32
    )
    rhs_data = lax.psum(rhs_part, "rows")
    noise_cols = lax.dynamic_slice_in_dim(coef_noise, eig_index * sample_share, sample_share, 1)
    rhs_all = rhs_data + noise_cols / jnp.sqrt(spectrum)[:, None]
    row_ids = row_index * row_share + jnp.arange(row_share, dtype=jnp.int32)
    col_ids = eig_index * width_dev + jnp.arange(width_dev, dtype=jnp.int32)
    inverse_prior = 1.0 / lax.dynamic_slice_in_dim(spectrum, row_index * row_share, row_share, 0)
    on_diagonal = row_ids[:, None] == col_ids[None, :]
    precision_block = gram_block + jnp.where(on_diagonal, inverse_prior[:, None], jnp.float32(0.0))
    panel_piece = from_root(precision_block[:, :PANEL], "eig", 0)
    panel = lax.all_gather(panel_piece, "rows", axis=0, tiled=True)
    head = jnp.linalg.cholesky(panel[:PANEL])
    every_factor_row = panel_factor_rows(head, panel, jnp.arange(order, dtype=jnp.int32))
    my_factor_rows = lax.dynamic_slice_in_dim(every_factor_row, row_index * row_share, row_share, 0)
    col_factor_rows = lax.dynamic_slice_in_dim(
        every_factor_row, eig_index * width_dev, width_dev, 0
    )
    schur = precision_block - jnp.dot(
        my_factor_rows, col_factor_rows.T, precision=lax.Precision.HIGHEST
    )
    panel_part = jnp.pad(my_factor_rows, ((0, 0), (0, width_dev - PANEL)))
    upper_zero = jnp.where(row_ids[:, None] < PANEL, jnp.float32(0.0), schur)
    factor = jnp.where(col_ids[None, :] < PANEL, panel_part, upper_zero)
    first = jax.scipy.linalg.solve_triangular(head, rhs_all[:PANEL], lower=True)
    my_rhs = lax.dynamic_slice_in_dim(rhs_all, row_index * row_share, row_share, 0)
    first_rows = jnp.take(first, jnp.clip(row_ids, 0, PANEL - 1), axis=0)
    updated = my_rhs - jnp.dot(my_factor_rows, first, precision=lax.Precision.HIGHEST)
    solved = jnp.where(row_ids[:, None] < PANEL, first_rows, updated)
    spectrum_block = lax.dynamic_slice_in_dim(spectrum, eig_index * width_dev, width_dev, 0)
    noise_block = lax.dynamic_slice_in_dim(coef_noise, eig_index * width_dev, width_dev, 0)
    scaled = (jnp.sqrt(spectrum_block)[:, None] * noise_block).astype(jnp.bfloat16)
    slab_prior = lax.psum_scatter(
        jnp.dot(phi_slab, scaled, preferred_element_type=jnp.float32),
        "eig",
        scatter_dimension=0,
        tiled=True,
    )
    return (factor, solved, slab_prior)


def solution(mesh):
    return jax.shard_map(
        on_device,
        mesh=mesh,
        in_specs=(P("rows", "eig"), P("rows"), P("rows", "eig"), P(), P(), P("rows", "eig")),
        out_specs=(P("rows", "eig"), P("rows", "eig"), P(("rows", "eig"), None)),
        check_vma=False,
    )
```

profile of v0, /device:TPU:1, one launch (start us, length us, event | category | flops | bytes accessed | tf_op | source)
XLA Modules:
  0.0 639.9 jit_solution(7270553847793615429)
XLA Ops:
  7.9 2.3 broadcast_multiply_fusion
  10.3 51.5 %all-gather.3.cloned.1.call-done = bf16[512,4096]{1,0:T(8,128)(2,1)} async-done(((bf16[512,1024]{1,0:T(8,128)(2,1)}), bf16[512,4096]{1,0:T(8,128)(2,1)}) %all-gather.3.cloned.1.call-update) | async-done | bytes 4194320 | tf_op jit(solution)/shard_map/all_gather | solution.py:37
  61.8 7.9 %broadcast_in_dim.87 = f32[4096,1024]{1,0:T(8,128)} broadcast(f32[]{:T(128)} %constant.218.clone.1), dimensions={} | broadcast | bytes 16777220 | tf_op jit(solution)/shard_map/broadcast_in_dim | solution.py:48
  69.7 29.1 %while.11 = (s32[]{:T(128)}, f32[4096,1024]{1,0:T(8,128)}, s32[]{:T(128)}, bf16[512,4096]{1,0:T(8,128)(2,1)}, bf16[512,1024]{1,0:T(8,128)(2,1)S(1)}, /*index=5*/s32[]{:T(128)}, s32[]{:T(128)}, s32[]{:T(128)}, s32[]{:T(128)}) while((s32[]{:T(128)}, f32[4096,1024]{1,0:T(8,128)}, s32[]{:T(128)}, bf16[512,4096]{1,0:T(8,128)(2,1)}, ...), condition=%wide.region_1.2_spmd, body=%wide.region_0.1_spmd.sunk | while | flops 2151677952 | bytes 36177032 | solution.py:48
  69.7 14.5 %convolution_add_fusion.2 = f32[4096,1024]{1,0:T(8,128)} fusion(f32[4096,1024]{1,0:T(8,128)} %get-tuple-element.159, bf16[512,4096]{1,0:T(8,128)(2,1)} %get-tuple-element.170, s32[]{:T(128)S(6)} %select_n.143, bf16[512,1024]{1,0:T(8,128)(2,1)S(1)} %get-tuple-element.171), kind=kOutput, calls=%fused_computation.2.clone.1 | convolution fusion | flops 2151677952 | bytes 36176896 | tf_op jit(solution)/shard_map/while/body/dot_general | solution.py:43
  84.3 14.5 %convolution_add_fusion.2 = f32[4096,1024]{1,0:T(8,128)} fusion(f32[4096,1024]{1,0:T(8,128)} %get-tuple-element.159, bf16[512,4096]{1,0:T(8,128)(2,1)} %get-tuple-element.170, s32[]{:T(128)S(6)} %select_n.143, bf16[512,1024]{1,0:T(8,128)(2,1)S(1)} %get-tuple-element.171), kind=kOutput, calls=%fused_computation.2.clone.1 | convolution fusion | flops 2151677952 | bytes 36176896 | tf_op jit(solution)/shard_map/while/body/dot_general | solution.py:43
  98.8 17.5 %copy.18 = f32[4096,1024]{0,1:T(8,128)} copy(f32[4096,1024]{1,0:T(8,128)} %get-tuple-element.31) | data formatting | bytes 33554432 | tf_op jit(solution)/shard_map/while | solution.py:48
  116.3 3.8 fusion.65
  120.9 177.5 %all-reduce.8.cloned.1.call-done = (f32[4096,1024]{0,1:T(8,128)}, f32[4096,32]{0,1:T(8,128)}) async-done(((f32[4096,1024]{0,1:T(8,128)}, f32[4096,32]{0,1:T(8,128)}), (f32[4096,1024]{0,1:T(8,128)}, f32[4096,32]{0,1:T(8,128)})) %all-reduce.8.cloned.1.call-update) | async-done | bytes 17301520 | tf_op jit(solution)/shard_map/psum | solution.py:47
  298.4 1.2 select_add_fusion
  301.2 5.2 convolution_bitcast_fusion
  306.6 35.3 %all-reduce.6.cloned.1.call-done = f32[128,512]{0,1:T(8,128)} async-done(((f32[128,512]{0,1:T(8,128)}), f32[128,512]{0,1:T(8,128)}) %all-reduce.6.cloned.1.call-update) | async-done | bytes 262160 | tf_op jit(solution)/shard_map/psum | solution.py:12
  342.0 2.2 constant_dynamic-slice_fusion.1
  344.9 24.4 %reduce-scatter.2.cloned.1.call-done = f32[512,128]{0,1:T(8,128)} async-done(((f32[2048,128]{0,1:T(8,128)}), f32[512,128]{0,1:T(8,128)}) %reduce-scatter.2.cloned.1.call-update) | async-done | bytes 262160 | tf_op jit(solution)/shard_map/reduce_scatter | solution.py:84
  369.3 1.8 copy.26
  371.9 59.5 %all-gather.5.cloned.1.call-done = f32[4096,512]{0,1:T(8,128)} async-done(((f32[128,512]{0,1:T(8,128)}), f32[4096,512]{0,1:T(8,128)}) %all-gather.5.cloned.1.call-update) | async-done | bytes 8388624 | tf_op jit(solution)/shard_map/all_gather | solution.py:63
  431.4 1.3 slice.176
  433.1 1.4 fusion.30
  434.5 11.7 %cholesky.106 = f32[128,128]{1,0:T(8,128)S(1)} custom-call(f32[128,128]{1,0:T(8,128)S(1)} %cholesky.272), custom_call_target="Cholesky" | custom-call | tf_op jit(solution)/shard_map/jit(cholesky)/cholesky | solution.py:64
  446.4 9.8 %custom-call.34 = f32[1,128,128]{1,2,0:T(8,128)S(1)} custom-call(f32[1,128,128]{2,1,0:T(8,128)S(1)} %get-tuple-element.79), custom_call_target="InvertDiagBlocksLowerTriangular" | custom-call | tf_op jit(solution)/shard_map/jit(cholesky)/cholesky | solution.py:64
  456.9 12.1 %cholesky.221 = f32[128,128]{1,0:T(8,128)S(1)} custom-call(f32[128,128]{1,0:T(8,128)S(1)} %cholesky.276), custom_call_target="Cholesky" | custom-call | tf_op jit(solution)/shard_map/jit(cholesky)/cholesky | solution.py:64
  469.1 9.8 %custom-call.35 = f32[1,128,128]{1,2,0:T(8,128)S(1)} custom-call(f32[1,128,128]{2,1,0:T(8,128)S(1)} %get-tuple-element.76), custom_call_target="InvertDiagBlocksLowerTriangular" | custom-call | tf_op jit(solution)/shard_map/jit(cholesky)/cholesky | solution.py:64
  479.5 11.7 %cholesky.242 = f32[128,128]{1,0:T(8,128)S(1)} custom-call(f32[128,128]{1,0:T(8,128)S(1)} %cholesky.281), custom_call_target="Cholesky" | custom-call | tf_op jit(solution)/shard_map/jit(cholesky)/cholesky | solution.py:64
  492.0 9.8 %custom-call.36 = f32[1,128,128]{1,2,0:T(8,128)S(1)} custom-call(f32[1,128,128]{2,1,0:T(8,128)S(1)} %get-tuple-element.73), custom_call_target="InvertDiagBlocksLowerTriangular" | custom-call | tf_op jit(solution)/shard_map/jit(cholesky)/cholesky | solution.py:64
  502.4 11.8 %cholesky.259 = f32[128,128]{1,0:T(8,128)S(1)} custom-call(f32[128,128]{1,0:T(8,128)S(1)} %convolution_subtract_fusion.4), custom_call_target="Cholesky" | custom-call | tf_op jit(solution)/shard_map/jit(cholesky)/cholesky | solution.py:64
  518.6 8.3 %while.12 = (s32[]{:T(128)}, f32[512,512]{1,0:T(8,128)S(1)}, s32[4,2]{0,1:T(2,128)S(1)}, f32[4,128,128]{2,1,0:T(8,128)S(1)}, s32[]{:T(128)}) while((s32[]{:T(128)}, f32[512,512]{1,0:T(8,128)S(1)}, s32[4,2]{0,1:T(2,128)S(1)}, f32[4,128,128]{2,1,0:T(8,128)S(1)}, s32[]{:T(128)}) %tuple.52), condition=%wide.while_cond, body=%wide.while_body.sunk | while | flops 2 | bytes 131181 | solution.py:16
  519.2 1.4 bitcast_dynamic-update-slice_fusion.2
  521.3 1.4 bitcast_dynamic-update-slice_fusion.2
  523.4 1.4 bitcast_dynamic-update-slice_fusion.2
  525.4 1.4 bitcast_dynamic-update-slice_fusion.2
  526.9 39.3 %custom-call.37 = f32[4,128,128]{1,2,0:T(8,128)S(1)} custom-call(f32[4,128,128]{2,1,0:T(8,128)S(1)} %get-tuple-element.39), custom_call_target="InvertDiagBlocksLowerTriangular" | custom-call | tf_op jit(solution)/shard_map/jit(_solve_triangular)/triangular_solve | solution.py:16
  567.1 0.9 convolution_subtract_fusion.8
  568.2 1.0 convolution_subtract_fusion.7
  569.3 1.0 convolution_subtract_fusion.6
  571.4 16.8 %gather_fusion = f32[4096,512]{1,0:T(8,128)} fusion(f32[512,512]{1,0:T(8,128)S(1)} %get-tuple-element.67, s32[4096]{0:T(1024)S(1)} %broadcast_clamp_fusion), kind=kCustom, calls=%fused_computation | custom fusion | bytes 16793600 | tf_op jit(solution)/shard_map/jit(_take)/gather | solution.py:17
  588.2 8.9 %copy.20 = f32[4096,512]{0,1:T(8,128)} copy(f32[4096,512]{1,0:T(8,128)} %gather_fusion) | data formatting | bytes 16777216 | tf_op jit(solution)/shard_map/jit(_take)/gather | solution.py:17
  597.1 3.5 fusion.16
  600.6 3.5 convolution_subtract_fusion.1
  604.2 2.0 fusion.50
  606.1 4.0 convolution_subtract_fusion
  610.2 2.0 fusion.52
  612.2 5.9 fusion.10
  618.1 1.9 fusion.54
  620.1 4.2 fusion.3
  624.3 1.0 constant_dynamic-slice_fusion.2
  625.2 5.1 fusion.26
  630.3 1.0 copy.25
  631.3 1.8 fusion.29
  (81 shorter events, 13.9 us)
Async XLA Ops:
  7.2 54.7 %all-gather.3.cloned.1.call-start = ((), (), s32[]{:S(2)}) async-start(), calls=%async_computation.1 | async-start | bytes 5242880 | tf_op jit(solution)/shard_map/all_gather | solution.py:37
  10.2 288.1 %all-reduce.8.cloned.1.call-start = ((), (), s32[]{:S(2)}) async-start(), calls=%async_computation.5 | async-start | bytes 34603008 | tf_op jit(solution)/shard_map/psum | solution.py:47
  10.3 59.4 %copy-start = (bf16[512,1024]{1,0:T(8,128)(2,1)S(1)}, bf16[512,1024]{1,0:T(8,128)(2,1)}, u32[]{:S(2)}) copy-start(bf16[512,1024]{1,0:T(8,128)(2,1)} %broadcast_multiply_fusion) | copy-start | bytes 3145732
  98.8 17.5 %copy-start.4 = (bf16[512,32]{0,1:T(8,128)(2,1)S(1)}, bf16[512,32]{0,1:T(8,128)(2,1)}, u32[]{:S(2)}) copy-start(bf16[512,32]{0,1:T(8,128)(2,1)} %param.10) | copy-start | bytes 98308
  120.1 0.7 copy-start.5
  120.1 221.8 %all-reduce.6.cloned.1.call-start = ((), (), s32[]{:S(2)}) async-start(), calls=%async_computation.2 | async-start | bytes 524288 | tf_op jit(solution)/shard_map/psum | solution.py:12
  299.6 0.8 copy-start.1
  301.2 68.1 %reduce-scatter.2.cloned.1.call-start = ((), (), s32[]{:S(2)}) async-start(), calls=%async_computation.4 | async-start | bytes 1310720 | tf_op jit(solution)/shard_map/reduce_scatter | solution.py:84
  306.4 64.7 %copy-start.3 = (f32[4096,32]{0,1:T(8,128)S(1)}, f32[4096,32]{0,1:T(8,128)}, u32[]{:S(2)}) copy-start(f32[4096,32]{0,1:T(8,128)} %get-tuple-element.65) | copy-start | bytes 1572868
  306.4 125.0 %all-gather.5.cloned.1.call-start = ((), (), s32[]{:S(2)}) async-start(), calls=%async_computation.3 | async-start | bytes 8650752 | tf_op jit(solution)/shard_map/all_gather | solution.py:63
  610.2 9.9 %slice-start = ((s8[8388608]{0:T(1024)(128)(4,1)}), s8[4194304]{0:T(1024)(128)(4,1)S(1)}, s32[]{:S(2)}) async-start(s8[8388608]{0:T(1024)(128)(4,1)} %bitcast.72), calls=%async_computation.6 | async-start | bytes 8388608
  612.2 7.9 %slice-start.1 = ((s8[8388608]{0:T(1024)(128)(4,1)}), s8[4194304]{0:T(1024)(128)(4,1)S(1)}, s32[]{:S(2)}) async-start(s8[8388608]{0:T(1024)(128)(4,1)} %bitcast.72), calls=%async_computation.7 | async-start | bytes 8388608
  620.1 5.1 copy-start.2
Sparse Core Ops, SparseCore 0:
  10.3 51.4 all-gather.2
  120.2 178.0 all-reduce.7
  301.3 40.6 all-reduce.5
  344.2 25.0 reduce-scatter.1
  371.3 60.1 all-gather.4
where the time goes:
time: 646 us; the launch traced here: 640 us
  waiting for transfers between devices  348 us (54%)
  other arithmetic  130 us (20%)
  matrix products  74 us (11%)
  local copies, waits for them, and re-layouts  69.8 us (11%)
  between operations  17.8 us (3%)
    psum x1, waiting for transfers between devices, on_device(): lax.psum(lax.fori_loop(0, block_count, add_block, jnp.zeros((order, width...  177 us
    another operation x14, other arithmetic, on_device(): head = jnp.linalg.cholesky(panel[:PANEL])  79 us
    all_gather x1, waiting for transfers between devices, on_device(): panel = lax.all_gather(panel_piece, 'rows', axis=0, tiled=True)  59.5 us
    all_gather x1, waiting for transfers between devices, on_device(): full_rows = lax.all_gather(local_rows, 'eig', axis=1, tiled=True)  51.5 us
    another operation x3, other arithmetic, panel_factor_rows(): jax.scipy.linalg.solve_triangular(head, panel_rows.T, lower=True)  39.6 us
    psum x1, waiting for transfers between devices, from_root(): return lax.psum(jnp.where(mine, array, jnp.zeros_like(array)), axis)  35.3 us
    dot_general x2, matrix products, add_block(): lax.dot_general(left, right, (((0,), (0,)), ((), ())), preferred_element_...  29.1 us
    gather x2, local copies, waits for them, and re-layouts, panel_factor_rows(): head_rows = jnp.take(head, jnp.clip(row_ids, 0, head.shape[0] - 1), axis=0)  25.7 us
  transfers between devices with their start and end apart: 5, of which 5 were waited for; matrix products, arithmetic and copies ran while one was open for 2% of the time, Pallas kernels for 0%

commit v1 on v0

v1 whole, which is shorter than its diff:
```python
import jax
import jax.numpy as jnp
from jax import lax
from jax.sharding import PartitionSpec as P

PANEL = 512
BLOCK = 128
EXACT = lax.Precision.HIGHEST


def contract_rows(left, right):
    return lax.dot_general(
        left, right, (((0,), (0,)), ((), ())), preferred_element_type=jnp.float32
    )


def mul(left, right):
    return jnp.dot(left, right, precision=EXACT)


def factor_head(head_matrix):
    steps = PANEL // BLOCK
    eye = jnp.eye(BLOCK, dtype=jnp.float32)
    remaining = head_matrix
    columns = []
    inverse_rows = []
    for step in range(steps):
        diagonal = jnp.linalg.cholesky(remaining[:BLOCK, :BLOCK], symmetrize_input=False)
        inverse = jax.scipy.linalg.solve_triangular(diagonal, eye, lower=True)
        column = diagonal
        if step + 1 < steps:
            below = mul(remaining[BLOCK:, :BLOCK], inverse.T)
            remaining = remaining[BLOCK:, BLOCK:] - mul(below, below.T)
            column = jnp.concatenate([diagonal, below], axis=0)
        columns.append(column)
        row = inverse
        if step:
            left = jnp.concatenate(
                [
                    columns[c][(step - c) * BLOCK : (step - c + 1) * BLOCK]
                    for c in range(step)
                ],
                axis=1,
            )
            above = jnp.concatenate(
                [jnp.pad(r, ((0, 0), (0, step * BLOCK - r.shape[1]))) for r in inverse_rows],
                axis=0,
            )
            row = jnp.concatenate([-mul(mul(inverse, left), above), inverse], axis=1)
        inverse_rows.append(row)
    head = jnp.concatenate(
        [jnp.pad(c, ((PANEL - c.shape[0], 0), (0, 0))) for c in columns], axis=1
    )
    head_inverse = jnp.concatenate(
        [jnp.pad(r, ((0, 0), (0, PANEL - r.shape[1]))) for r in inverse_rows], axis=0
    )
    return head, head_inverse


def on_device(phi_obs, counts, targets, spectrum, coef_noise, phi_slab):
    rows_total = lax.axis_size("rows")
    eig_total = lax.axis_size("eig")
    row_index = lax.axis_index("rows")
    eig_index = lax.axis_index("eig")
    obs_slots, width_dev = phi_obs.shape
    order = width_dev * eig_total
    row_share = order // rows_total
    rows_per_eig = rows_total // eig_total
    sample_share = targets.shape[1]
    slab_share = phi_slab.shape[0] // eig_total
    position = jnp.arange(obs_slots, dtype=jnp.int32)
    keep = (position < counts[0])[:, None]
    local_rows = jnp.where(keep, phi_obs, jnp.zeros_like(phi_obs))
    local_targets = jnp.where(keep, targets, jnp.zeros_like(targets))
    full_rows = lax.all_gather(local_rows, "eig", axis=1, tiled=True)

    spectrum_block = lax.dynamic_slice_in_dim(spectrum, eig_index * width_dev, width_dev, 0)
    noise_block = lax.dynamic_slice_in_dim(coef_noise, eig_index * width_dev, width_dev, 0)
    scaled = (jnp.sqrt(spectrum_block)[:, None] * noise_block).astype(jnp.bfloat16)
    slab_part = jnp.dot(phi_slab, scaled, preferred_element_type=jnp.float32)

    def slab_piece(owner):
        return lax.dynamic_slice_in_dim(slab_part, owner * slab_share, slab_share, 0)

    slab_prior = slab_piece(eig_index)
    for shift in range(1, eig_total):
        ring = [(e, (e + shift) % eig_total) for e in range(eig_total)]
        owner = (eig_index + shift) % eig_total
        slab_prior = slab_prior + lax.ppermute(slab_piece(owner), "eig", ring)

    panel_cols = full_rows[:, :PANEL]
    head_part = contract_rows(panel_cols, panel_cols)
    rhs_part = contract_rows(local_targets, full_rows)
    head_gram, rhs_data = lax.psum((head_part, rhs_part), "rows")
    panel_part = contract_rows(panel_cols, local_rows)
    panel_piece = lax.psum_scatter(panel_part, "rows", scatter_dimension=0, tiled=True)
    panel_gram = lax.all_gather(panel_piece, "rows", axis=0, tiled=True)
    gram_part = contract_rows(full_rows, local_rows)
    gram_block = lax.psum_scatter(gram_part, "rows", scatter_dimension=0, tiled=True)

    inverse_prior = 1.0 / spectrum
    col_ids = eig_index * width_dev + jnp.arange(width_dev, dtype=jnp.int32)
    row_ids = row_index * row_share + jnp.arange(row_share, dtype=jnp.int32)
    panel_ids = jnp.arange(PANEL, dtype=jnp.int32)
    zero = jnp.float32(0.0)
    prior_head = inverse_prior[:PANEL, None]
    head_matrix = head_gram + jnp.where(
        panel_ids[:, None] == panel_ids[None, :], prior_head, zero
    )
    panel = panel_gram + jnp.where(panel_ids[:, None] == col_ids[None, :], prior_head, zero)

    own_piece = lax.dynamic_slice_in_dim(
        panel, (row_index % rows_per_eig) * row_share, row_share, 1
    )
    row_panel = jnp.where(eig_index == row_index // rows_per_eig, own_piece, zero)
    for shift in range(1, eig_total):
        pairs = []
        for r in range(rows_total):
            source = r // rows_per_eig
            target = (source + shift) % eig_total
            pairs.append((r * eig_total + source, r * eig_total + target))
        row_panel = row_panel + lax.ppermute(own_piece, ("rows", "eig"), pairs)

    head, head_inverse = factor_head(head_matrix)
    solved_cols = mul(head_inverse, panel)
    solved_rows = mul(head_inverse, row_panel)
    noise_cols = lax.dynamic_slice_in_dim(coef_noise, eig_index * sample_share, sample_share, 1)
    rhs_all = rhs_data + (noise_cols / jnp.sqrt(spectrum)[:, None]).T
    first = mul(rhs_all[:, :PANEL], head_inverse.T)
    in_head = row_index * row_share < PANEL
    head_start = jnp.minimum(row_index * row_share, PANEL - row_share)
    head_rows = lax.dynamic_slice_in_dim(head, head_start, row_share, 0)
    first_rows = lax.dynamic_slice_in_dim(first, head_start, row_share, 1)
    my_rhs = lax.dynamic_slice_in_dim(rhs_all, row_index * row_share, row_share, 1)
    solved = jnp.where(in_head, first_rows, my_rhs - mul(first, solved_rows)).T
    my_factor_rows = jnp.where(in_head, head_rows, solved_rows.T)
    update = mul(solved_rows.T, solved_cols)
    my_prior = lax.dynamic_slice_in_dim(inverse_prior, row_index * row_share, row_share, 0)
    on_diagonal = row_ids[:, None] == col_ids[None, :]
    schur = gram_block + jnp.where(on_diagonal, my_prior[:, None], zero) - update
    panel_out = jnp.pad(my_factor_rows, ((0, 0), (0, width_dev - PANEL)))
    trailing = jnp.where(in_head, zero, schur)
    factor = jnp.where(col_ids[None, :] < PANEL, panel_out, trailing)
    return (factor, solved, slab_prior)


def solution(mesh):
    return jax.shard_map(
        on_device,
        mesh=mesh,
        in_specs=(P("rows", "eig"), P("rows"), P("rows", "eig"), P(), P(), P("rows", "eig")),
        out_specs=(P("rows", "eig"), P("rows", "eig"), P(("rows", "eig"), None)),
        check_vma=False,
    )
```

time: 646 us -> 434 us (0.67)
  waiting for transfers between devices: 348 us -> 247 us
  local copies, waits for them, and re-layouts: 69.8 us -> 9.1 us
  matrix products: 74 us -> 41.8 us
  other arithmetic: 130 us -> 102 us
  starting transfers between devices: 0.38 us -> 12.4 us
    psum x2 -> x1, waiting for transfers between devices: 213 us -> 79.9 us  [on_device(): head_gram, rhs_data = lax.psum((head_part, rhs_part), 'rows')]
    reduce_scatter x1 -> x2, waiting for transfers between devices: 24.4 us -> 110 us  [the longest x1 70.9 us: on_device(): lax.psum_scatter(panel_part, 'rows', scatter_dimension=0, tiled=True)]
    all_gather x1, waiting for transfers between devices: 59.5 us -> 0.01 us  [on_device(): panel_gram = lax.all_gather(panel_piece, 'rows', axis=0, tiled=True)]
    another operation x20 -> x4, matrix products: 29.1 us -> 1.08 us  [factor_head(): inverse = jax.scipy.linalg.solve_triangular(diagonal, eye, lower=True)]
    another operation x18 -> x20, other arithmetic: 119 us -> 92 us  [the longest x12 50.1 us: factor_head(): jnp.linalg.cholesky(remaining[:BLOCK, :BLOCK], symmetrize_input=False)]
    gather x4 -> x0, local copies, waits for them, and re-layouts: 26.4 us -> none  [the longest x2 25.7 us: panel_factor_rows(): head_rows = jnp.take(head, jnp.clip(row_ids, 0, head.shape[0] - 1), axis=0)]
    while x1 -> x0, local copies, waits for them, and re-layouts: 17.5 us -> none  [on_device(): lax.fori_loop(0, block_count, add_block, jnp.zeros((order, width_dev), jn...]
    ppermute x0 -> x6, starting transfers between devices: none -> 12.2 us  [the longest x3 7.08 us: on_device(): row_panel = row_panel + lax.ppermute(own_piece, ('rows', 'eig'), pairs)]
  transfers between devices with their start and end apart: 5 -> 11, of which waited for: 5 -> 6; matrix products, arithmetic and copies ran while one was open for 2% -> 33% of each run, Pallas kernels for 0% -> 0%
where the time goes in v1:
time: 434 us; the launch traced here: 427 us
  waiting for transfers between devices  247 us (57%)
  other arithmetic  102 us (24%)
  matrix products  41.8 us (10%)
  between operations  15.2 us (4%)
  starting transfers between devices  12.4 us (3%)
  local copies, waits for them, and re-layouts  9.1 us (2%)
    psum x1, waiting for transfers between devices, on_device(): head_gram, rhs_data = lax.psum((head_part, rhs_part), 'rows')  79.9 us
    reduce_scatter x1, waiting for transfers between devices, on_device(): lax.psum_scatter(panel_part, 'rows', scatter_dimension=0, tiled=True)  70.9 us
    all_gather x1, waiting for transfers between devices, on_device(): full_rows = lax.all_gather(local_rows, 'eig', axis=1, tiled=True)  51.6 us
    another operation x12, other arithmetic, factor_head(): jnp.linalg.cholesky(remaining[:BLOCK, :BLOCK], symmetrize_input=False)  50.1 us
    another operation x8, other arithmetic, factor_head(): inverse = jax.scipy.linalg.solve_triangular(diagonal, eye, lower=True)  41.9 us
    reduce_scatter x1, waiting for transfers between devices, on_device(): lax.psum_scatter(gram_part, 'rows', scatter_dimension=0, tiled=True)  38.9 us
    dot_general x4, matrix products, contract_rows(): lax.dot_general(left, right, (((0,), (0,)), ((), ())), preferred_element_...  20.5 us
    dot_general x17, matrix products, mul(): return jnp.dot(left, right, precision=EXACT)  16.1 us
  transfers between devices with their start and end apart: 11, of which 6 were waited for; matrix products, arithmetic and copies ran while one was open for 33% of the time, Pallas kernels for 0%

profile of v1, /device:TPU:1, one launch (start us, length us, event | category | flops | bytes accessed | tf_op | source)
XLA Modules:
  0.0 427.4 jit_solution(798537315321918684)
XLA Ops:
  7.9 2.3 broadcast_select_fusion
  10.3 51.6 %all-gather.3.cloned.1.call-done = bf16[512,4096]{1,0:T(8,128)(2,1)} async-done(((bf16[512,1024]{1,0:T(8,128)(2,1)}), bf16[512,4096]{1,0:T(8,128)(2,1)}) %all-gather.3.cloned.1.call-update) | async-done | bytes 4194320 | tf_op jit(solution)/shard_map/all_gather | solution.py:75
  61.8 3.5 fusion.17
  65.4 2.8 fusion.19
  68.1 3.9 fusion.79
  72.1 70.9 %reduce-scatter.3.cloned.1.call-done = f32[16,1024]{1,0:T(8,128)} async-done(((f32[512,1024]{1,0:T(8,128)}), f32[16,1024]{1,0:T(8,128)}) %reduce-scatter.3.cloned.1.call-update) | async-done | bytes 65552 | tf_op jit(solution)/shard_map/reduce_scatter | solution.py:96
  143.1 10.4 %fusion.102 = f32[4096,1024]{1,0:T(8,128)} fusion(bf16[512,4096]{1,0:T(8,128)(2,1)} %all-gather.3.cloned.1.call-done, bf16[512,1024]{1,0:T(8,128)(2,1)S(1)} %copy-done), kind=kOutput, calls=%fused_computation.165 | convolution fusion | flops 4294967296 | bytes 22020096 | tf_op jit(solution)/shard_map/dot_general | solution.py:12
  153.5 0.6 copy-done.10
  154.1 4.1 fusion.24
  158.3 0.9 dynamic-slice_bitcast_fusion.2
  159.2 1.3 collective-permute-start.3
  160.4 2.6 collective-permute-start.4
  163.0 1.3 collective-permute-start.5
  164.3 2.2 constant_dynamic-slice_fusion
  167.0 1.4 copy.20
  168.4 0.7 dynamic_slice.38
  170.2 2.5 collective-permute-done.4
  172.6 1.2 fusion.36
  173.8 0.8 copy.18
  174.7 79.9 %all-reduce.13.cloned.1.call-done = (f32[512,512]{1,0:T(8,128)}, f32[32,4096]{1,0:T(8,128)}) async-done(((f32[512,512]{1,0:T(8,128)}, f32[32,4096]{1,0:T(8,128)}), (f32[512,512]{1,0:T(8,128)}, f32[32,4096]{1,0:T(8,128)})) %all-reduce.13.cloned.1.call-update) | async-done | bytes 1572880 | tf_op jit(solution)/shard_map/psum | solution.py:94
  254.6 1.4 select_add_fusion.1
  256.0 11.7 %cholesky.75 = f32[128,128]{1,0:T(8,128)S(1)} custom-call(f32[128,128]{1,0:T(8,128)S(1)} %slice.78), custom_call_target="Cholesky" | custom-call | tf_op jit(solution)/shard_map/jit(cholesky)/cholesky | solution.py:28
  268.4 0.7 select_bitcast_fusion.3
  269.1 9.8 %custom-call.8 = f32[1,128,128]{1,2,0:T(8,128)S(1)} custom-call(f32[1,128,128]{2,1,0:T(8,128)S(1)} %get-tuple-element.16), custom_call_target="InvertDiagBlocksLowerTriangular" | custom-call | tf_op jit(solution)/shard_map/jit(_solve_triangular)/triangular_solve | solution.py:29
  279.6 0.8 copy.9
  280.4 0.7 convolution_subtract_fusion
  281.1 11.9 %cholesky.86 = f32[128,128]{1,0:T(8,128)S(1)} custom-call(f32[128,128]{1,0:T(8,128)S(1)} %slice.81), custom_call_target="Cholesky" | custom-call | tf_op jit(solution)/shard_map/jit(cholesky)/cholesky | solution.py:28
  293.6 0.7 select_bitcast_fusion.2
  294.3 9.8 %custom-call.9 = f32[1,128,128]{1,2,0:T(8,128)S(1)} custom-call(f32[1,128,128]{2,1,0:T(8,128)S(1)} %get-tuple-element.14), custom_call_target="InvertDiagBlocksLowerTriangular" | custom-call | tf_op jit(solution)/shard_map/jit(_solve_triangular)/triangular_solve | solution.py:29
  305.3 11.7 %cholesky.97 = f32[128,128]{1,0:T(8,128)S(1)} custom-call(f32[128,128]{1,0:T(8,128)S(1)} %slice.84), custom_call_target="Cholesky" | custom-call | tf_op jit(solution)/shard_map/jit(cholesky)/cholesky | solution.py:28
  317.7 0.7 select_bitcast_fusion.1
  318.4 9.8 %custom-call.10 = f32[1,128,128]{1,2,0:T(8,128)S(1)} custom-call(f32[1,128,128]{2,1,0:T(8,128)S(1)} %get-tuple-element.12), custom_call_target="InvertDiagBlocksLowerTriangular" | custom-call | tf_op jit(solution)/shard_map/jit(_solve_triangular)/triangular_solve | solution.py:29
  329.2 12.1 %cholesky.108 = f32[128,128]{1,0:T(8,128)S(1)} custom-call(f32[128,128]{1,0:T(8,128)S(1)} %convolution_subtract_fusion.3), custom_call_target="Cholesky" | custom-call | tf_op jit(solution)/shard_map/jit(cholesky)/cholesky | solution.py:28
  342.0 0.7 select_bitcast_fusion
  342.6 9.8 %custom-call.11 = f32[1,128,128]{1,2,0:T(8,128)S(1)} custom-call(f32[1,128,128]{2,1,0:T(8,128)S(1)} %get-tuple-element.10), custom_call_target="InvertDiagBlocksLowerTriangular" | custom-call | tf_op jit(solution)/shard_map/jit(_solve_triangular)/triangular_solve | solution.py:29
  355.3 0.8 copy-done.2
  356.1 1.4 fusion.69
  357.5 2.1 select_add_fusion
  359.7 3.3 collective-permute-start
  363.0 2.3 collective-permute-start.1
  365.3 1.5 collective-permute-start.2
  366.8 3.5 fusion.96
  370.4 3.4 collective-permute-done.1
  373.7 2.0 fusion.38
  375.9 1.7 fusion.3
  377.6 1.0 fusion.29
  378.6 38.9 %reduce-scatter.5.cloned.1.call-done = f32[128,1024]{1,0:T(8,128)} async-done(((f32[4096,1024]{1,0:T(8,128)}), f32[128,1024]{1,0:T(8,128)}) %reduce-scatter.5.cloned.1.call-update) | async-done | bytes 524304 | tf_op jit(solution)/shard_map/reduce_scatter | solution.py:99
  417.5 3.2 fusion.1
  (92 shorter events, 10.3 us)
Async XLA Ops:
  7.2 54.7 %all-gather.3.cloned.1.call-start = ((), (), s32[]{:S(2)}) async-start(), calls=%async_computation.2 | async-start | bytes 5242880 | tf_op jit(solution)/shard_map/all_gather | solution.py:75
  10.2 132.7 %reduce-scatter.3.cloned.1.call-start = ((), (), s32[]{:S(2)}) async-start(), calls=%async_computation.3 | async-start | bytes 2162688 | tf_op jit(solution)/shard_map/reduce_scatter | solution.py:96
  65.3 2.8 copy-start.9
  65.3 189.3 %all-reduce.13.cloned.1.call-start = ((), (), s32[]{:S(2)}) async-start(), calls=%async_computation.6 | async-start | bytes 3145728 | tf_op jit(solution)/shard_map/psum | solution.py:94
  68.1 74.9 %copy-start = (bf16[512,1024]{1,0:T(8,128)(2,1)S(1)}, bf16[512,1024]{1,0:T(8,128)(2,1)}, u32[]{:S(2)}) copy-start(bf16[512,1024]{1,0:T(8,128)(2,1)} %broadcast_select_fusion) | copy-start | bytes 3145732
  72.1 285.4 %all-gather.5.cloned.1.call-start = ((), (), s32[]{:S(2)}) async-start(), calls=%async_computation.4 | async-start | bytes 2162688 | tf_op jit(solution)/shard_map/all_gather | solution.py:97
  143.0 274.5 %reduce-scatter.5.cloned.1.call-start = ((), (), s32[]{:S(2)}) async-start(), calls=%async_computation.5 | async-start | bytes 17301504 | tf_op jit(solution)/shard_map/reduce_scatter | solution.py:99
  153.4 0.7 copy-start.10
  159.2 11.0 %collective-permute-start.3 = (f32[512,128]{0,1:T(8,128)}, f32[512,128]{0,1:T(8,128)}, u32[]{:S(2)}, u32[]{:S(2)}) collective-permute-start(f32[512,128]{0,1:T(8,128)} %get-tuple-element.18), channel_id=1, source_target_pairs={{0,1},{1,2},{2,3},{3,0},{4,5},{5,6},{6,7},{7,4},{8,9},{9,10},{10,1... | collective-permute-start | bytes 786440 | tf_op jit(solution)/shard_map/ppermute | solution.py:89
  160.4 12.2 %collective-permute-start.4 = (f32[512,128]{0,1:T(8,128)}, f32[512,128]{0,1:T(8,128)}, u32[]{:S(2)}, u32[]{:S(2)}) collective-permute-start(f32[512,128]{0,1:T(8,128)} %get-tuple-element.20), channel_id=1, source_target_pairs={{0,2},{1,3},{2,0},{3,1},{4,6},{5,7},{6,4},{7,5},{8,10},{9,11},{10,... | collective-permute-start | bytes 786440 | tf_op jit(solution)/shard_map/ppermute | solution.py:89
  163.0 9.6 %collective-permute-start.5 = (f32[512,128]{0,1:T(8,128)S(1)}, f32[512,128]{0,1:T(8,128)}, u32[]{:S(2)}, u32[]{:S(2)}) collective-permute-start(f32[512,128]{0,1:T(8,128)S(1)} %get-tuple-element.19), channel_id=1, source_target_pairs={{0,3},{1,0},{2,1},{3,2},{4,7},{5,4},{6,5},{7,6},{8,11},{9,8},{10,9... | collective-permute-start | bytes 786440 | tf_op jit(solution)/shard_map/ppermute | solution.py:89
  167.0 87.6 %copy-start.11 = (f32[512]{0:T(512)}, f32[512]{0:T(512)S(1)}, u32[]{:S(2)}) copy-start(f32[512]{0:T(512)S(1)} %slice.77) | copy-start | bytes 6148
  352.8 2.5 copy-start.6
  353.3 1.9 copy-start.4
  354.0 1.0 copy-start.1
  354.0 1.2 copy-start.3
  355.0 11.8 %copy-start.16 = (f32[128,384]{1,0:T(8,128)}, f32[128,384]{1,0:T(8,128)S(1)}, u32[]{:S(2)}) copy-start(f32[128,384]{1,0:T(8,128)S(1)} %convolution_negate_fusion) | copy-start | bytes 589828
  355.3 0.8 copy-start.2
  356.1 1.4 copy-start.8
  356.1 1.4 copy-start.12
  357.5 9.3 %copy-start.5 = (f32[128,256]{1,0:T(8,128)S(1)}, f32[128,256]{1,0:T(8,128)}, u32[]{:S(2)}) copy-start(f32[128,256]{1,0:T(8,128)} %copy-done.4) | copy-start | bytes 393220
  357.5 9.3 %copy-start.7 = (f32[128,128]{1,0:T(8,128)S(1)}, f32[128,128]{1,0:T(8,128)}, u32[]{:S(2)}) copy-start(f32[128,128]{1,0:T(8,128)} %copy-done.6) | copy-start | bytes 196612
  359.7 10.7 %collective-permute-start = (f32[512,128]{1,0:T(8,128)S(1)}, f32[512,128]{1,0:T(8,128)S(1)}, u32[]{:S(2)}, u32[]{:S(2)}) collective-permute-start(f32[512,128]{1,0:T(8,128)S(1)} %constant_dynamic-slice_fusion.1), channel_id=1, source_target_pairs={{0,1},{4,5},{8,9},{12,13},{16,17},{20,21},{24,25},{28,29},{33,34},... | collective-permute-start | bytes 786440 | tf_op jit(solution)/shard_map/ppermute | solution.py:122
  363.0 10.7 %collective-permute-start.1 = (f32[512,128]{1,0:T(8,128)S(1)}, f32[512,128]{1,0:T(8,128)S(1)}, u32[]{:S(2)}, u32[]{:S(2)}) collective-permute-start(f32[512,128]{1,0:T(8,128)S(1)} %constant_dynamic-slice_fusion.1), channel_id=1, source_target_pairs={{0,2},{4,6},{8,10},{12,14},{16,18},{20,22},{24,26},{28,30},{33,35}... | collective-permute-start | bytes 786440 | tf_op jit(solution)/shard_map/ppermute | solution.py:122
  365.3 8.4 %collective-permute-start.2 = (f32[512,128]{1,0:T(8,128)S(1)}, f32[512,128]{1,0:T(8,128)S(1)}, u32[]{:S(2)}, u32[]{:S(2)}) collective-permute-start(f32[512,128]{1,0:T(8,128)S(1)} %constant_dynamic-slice_fusion.1), channel_id=1, source_target_pairs={{0,3},{4,7},{8,11},{12,15},{16,19},{20,23},{24,27},{28,31},{33,32}... | collective-permute-start | bytes 786440 | tf_op jit(solution)/shard_map/ppermute | solution.py:122
  375.7 41.8 %copy-start.13 = (pred[1024]{0:T(1024)(128)(4,1)S(1)}, pred[1024]{0:T(1024)(128)(4,1)}, u32[]{:S(2)}) copy-start(pred[1024]{0:T(1024)(128)(4,1)} %broadcast_compare_fusion) | copy-start | bytes 3076
  375.7 41.8 %copy-start.14 = (s32[128]{0:T(128)S(1)}, s32[128]{0:T(128)}, u32[]{:S(2)}) copy-start(s32[128]{0:T(128)} %iota_add_fusion.1) | copy-start | bytes 1540
  375.7 41.8 %copy-start.15 = (f32[128]{0:T(128)S(1)}, f32[128]{0:T(128)}, u32[]{:S(2)}) copy-start(f32[128]{0:T(128)} %dynamic_slice.38) | copy-start | bytes 1540
Sparse Core Ops, SparseCore 0:
  10.4 51.4 all-gather.2
  65.4 77.4 reduce-scatter.2
  146.9 107.6 all-reduce.12
  256.7 44.0 all-gather.4
  304.6 112.8 reduce-scatter.4
